TPU v7x, 512 devices: a whole 4x8x8 slice. The times are simulated.
512 devices in a mesh: dp: 16 (over x, z_hi), code: 32 (over z_lo, y, core).
Axes of the slice: x: 4, y: 8, z: 8 (z_hi: 4, z_lo: 2; z = z_hi * 2 + z_lo), core: 2. Of those that a mesh axis runs over, the one named last changes fastest.
Arguments:
- tokens: bfloat16 [8192, 256], P('dp'), may hold values from -40 to 40
- codebook: bfloat16 [131072, 256], P('code'), may hold values from -6 to 6
- cotangent: bfloat16 [8192, 256], P('dp'), may hold values from -6 to 6
- index: int32 [8192], P('dp'), may hold values from 0 to 131071
Outputs:
- quantized: bfloat16 [8192, 256], P('dp')
- token_grad: bfloat16 [8192, 256], P('dp')
- codebook_grad: bfloat16 [131072, 256], P(('code', 'dp'))
- code_usage: float32 [131072], P(('code', 'dp'))
- entropy_loss: float32 [], replicated
All inputs are finite; a program needn't handle non-finite values.
Results may differ from a plain program's by a relative error of at most 0.012.
Values may be sent and summed in bfloat16 or wider, within the bound.
A program may use at most 64 MiB of HBM per device.

v0:
```python
import jax
import jax.numpy as jnp
from jax import lax
from jax.sharding import PartitionSpec as P


def body(tokens, codebook, cotangent, index):
    token_rows, features = tokens.shape
    code_rows = codebook.shape[0]
    scale_factor = float(features) ** (-0.5)
    code_devices = lax.axis_size("code")
    data_devices = lax.axis_size("dp")
    offset = lax.axis_index("code") * code_rows
    block_length = min(1024, code_rows)
    block_count = code_rows // block_length
    stacked = codebook.reshape(block_count, block_length, features)
    local_ids = index - offset
    inside = (local_ids >= 0) & (local_ids < code_rows)
    picked = jnp.take(codebook, jnp.where(inside, local_ids, 0), axis=0)
    picked = jnp.where(inside[:, None], picked.astype(jnp.float32), 0.0)
    quantized = lax.psum(picked.astype(jnp.bfloat16), "code")
    chosen_sums = jax.ops.segment_sum(
        cotangent.astype(jnp.float32),
        jnp.where(inside, local_ids, code_rows),
        num_segments=code_rows + 1,
    )[:code_rows]

    def scores(code_block):
        logits = (
            jnp.einsum("td,kd->tk", tokens, code_block, preferred_element_type=jnp.float32)
            * scale_factor
        )
        sensed = jnp.einsum("td,kd->tk", cotangent, code_block, preferred_element_type=jnp.float32)
        return (logits, sensed)

    def block_totals(code_block):
        logits, sensed = scores(code_block)
        row_top = jnp.max(logits, axis=1)
        weights = jnp.exp(logits - row_top[:, None])
        return (
            row_top,
            jnp.sum(weights, axis=1),
            jnp.sum(weights * sensed, axis=1),
            jnp.sum(weights * logits, axis=1),
        )

    block_tops, block_sums, sensed_sums, logit_sums = lax.map(block_totals, stacked)
    local_peak = jnp.max(block_tops, axis=0)
    factor = jnp.exp(block_tops - local_peak[None, :])
    local_stats = (
        local_peak,
        jnp.sum(block_sums * factor, axis=0),
        jnp.sum(sensed_sums * factor, axis=0),
        jnp.sum(logit_sums * factor, axis=0),
    )
    row_peak = lax.pmax(local_stats[0], "code")
    rescale = jnp.exp(local_stats[0] - row_peak)
    row_total, sensed_total, logit_total = lax.psum(
        (local_stats[1] * rescale, local_stats[2] * rescale, local_stats[3] * rescale), "code"
    )
    row_dot = sensed_total / row_total
    token_entropy = jnp.log(row_total) + row_peak - logit_total / row_total

    def block_grads(code_block):
        logits, sensed = scores(code_block)
        probs = jnp.exp(logits - row_peak[:, None]) / row_total[:, None]
        logit_grad = (probs * (sensed - row_dot[:, None])).astype(jnp.bfloat16)
        return (probs, logit_grad)

    def gradient_step(running, code_block):
        probs, logit_grad = block_grads(code_block)
        running = running + jnp.dot(logit_grad, code_block, preferred_element_type=jnp.float32)
        usage_part = jnp.sum(probs, axis=0)
        grad_term = scale_factor * jnp.einsum(
            "tk,td->kd", logit_grad, tokens, preferred_element_type=jnp.float32
        )
        return (running, (usage_part, grad_term))

    running, outputs = lax.scan(
        gradient_step, jnp.zeros((token_rows, features), jnp.float32), stacked
    )
    usage_local = outputs[0].reshape(code_rows)
    code_local = outputs[1].reshape(code_rows, features) + chosen_sums
    code_sum = lax.psum_scatter(
        code_local.astype(jnp.bfloat16), "dp", scatter_dimension=0, tiled=True
    )
    usage_sum = lax.psum_scatter(usage_local, "dp", scatter_dimension=0, tiled=True)
    token_grad = (lax.psum(running, "code") * scale_factor).astype(jnp.bfloat16)
    tokens_total = token_rows * data_devices
    codes_total = code_rows * code_devices
    code_usage = usage_sum * (codes_total / tokens_total)
    shares = usage_sum / tokens_total
    local_loss = jnp.sum(token_entropy) / (tokens_total * code_devices) + jnp.sum(
        jax.scipy.special.xlogy(shares, shares)
    )
    entropy_loss = lax.psum(local_loss, ("dp", "code"))
    return (quantized, token_grad, code_sum, code_usage, entropy_loss)


def solution(mesh):
    placed = (P("dp", None), P("code", None), P("dp", None), P("dp"))
    return jax.shard_map(
        body,
        mesh=mesh,
        in_specs=placed,
        out_specs=(P("dp", None), P("dp", None), P(("code", "dp"), None), P(("code", "dp")), P()),
        check_vma=False,
    )
```

profile of v0, /device:TPU:1, one launch (start us, length us, event | category | flops | bytes accessed | tf_op | source)
XLA Modules:
  0.0 632.0 jit_solution(5439487695934471928)
XLA Ops:
  8.1 16.1 %while.31 = (s32[]{:T(128)}, f32[4,512]{1,0:T(4,128)S(1)}, f32[4,512]{1,0:T(4,128)S(1)}, f32[4,512]{1,0:T(4,128)S(1)}, f32[4,512]{1,0:T(4,128)S(1)}, /*index=5*/...) while((s32[]{:T(128)}, f32[4,512]{1,0:T(4,128)S(1)}, ...), condition=%wide.region_6.7_spmd, body=%wide.region_1.0_spmd.sunk | while | flops 542636032 | bytes 8941729 | solution.py:47
  8.1 1.6 multiply_reduce_fusion.5
  9.8 1.6 fusion.56
  12.2 1.6 multiply_reduce_fusion.5
  13.8 1.6 fusion.56
  16.2 1.6 multiply_reduce_fusion.5
  17.8 1.6 fusion.56
  20.2 1.6 multiply_reduce_fusion.5
  21.9 1.6 fusion.56
  24.2 59.2 %pmax.7 = f32[512]{0:T(512)S(1)} all-reduce(f32[512]{0:T(512)S(1)} %reduce_max.18), channel_id=1, replica_groups=mesh['dp'=16,'code'=32] {'code'}, use_global_device_ids=true, to_apply=%region_8.9 | all-reduce | flops 512 | bytes 4096 | tf_op jit(solution)/shard_map/pmax | solution.py:56
  83.5 53.9 %all-reduce.1 = (f32[512]{0:T(512)S(1)}, f32[512]{0:T(512)S(1)}, f32[512]{0:T(512)S(1)}) all-reduce(f32[512]{0:T(512)S(1)} %get-tuple-element.198, f32[512]{0:T(512)S(1)} %get-tuple-element.197, f32[512]{0:T(512)S(1)} %get-tuple-element.196), channel_id=1, replica_groups=mesh['dp'=16,'code'=32] {'code'}, use_global_device_ids=true, to_apply=%region_10.11 | all-reduce | flops 1536 | bytes 12288 | tf_op jit(solution)/shard_map/psum | solution.py:58
  138.0 24.0 %while.32 = (s32[]{:T(128)}, f32[512,256]{1,0:T(8,128)}, f32[4,1024]{1,0:T(4,128)S(1)}, f32[4,1024,256]{2,1,0:T(8,128)}, bf16[4,1024,256]{2,1,0:T(8,128)(2,1)}, ...) while((s32[]{:T(128)}, f32[512,256]{1,0:T(8,128)}, ...), condition=%wide.region_15.16_spmd.clone, body=%wide.region_13.15_spmd.clone.sunk | while | flops 1077935104 | bytes 22300912 | solution.py:79
  138.0 1.9 fusion.64
  141.8 1.5 fusion.65
  143.3 1.9 fusion.64
  145.8 2.3 convolution_add_fusion.2
  148.1 1.4 fusion.65
  149.5 1.9 fusion.64
  152.0 2.3 convolution_add_fusion.2
  154.3 1.5 fusion.65
  155.8 1.9 fusion.64
  158.3 2.3 convolution_add_fusion.2
  160.6 1.4 fusion.65
  162.2 3.4 gather_fusion
  166.6 6.4 %scatter_custom_fusion = f32[4097,256]{1,0:T(8,128)} fusion(s32[512]{0:T(512)S(1)} %subtract_select_fusion, f32[]{:T(128)} %constant.46.clone.1, bf16[512,256]{1,0:T(8,128)(2,1)S(1)} %copy-done.3), kind=kCustom, calls=%fused_computation.34 | custom fusion | flops 262144 | bytes 4457476 | tf_op jit(solution)/shard_map/scatter-add | solution.py:22
  173.0 5.3 fusion.22
  180.9 72.7 %all-reduce = f32[4096]{0:T(1024)S(1)} all-reduce(f32[4096]{0:T(1024)S(1)} %bitcast.105), channel_id=3, replica_groups=mesh['dp'=16,'code'=32] {'dp'}, use_global_device_ids=true, to_apply=%region_19.20.clone | all-reduce | flops 4096 | bytes 32768
  255.4 107.1 %psum.47 = f32[]{:T(128)} all-reduce(f32[]{:T(128)S(6)} %add.45), channel_id=1, replica_groups=mesh['dp'=16,'code'=32] {'dp','code'}, use_global_device_ids=true, to_apply=%region_24.25 | all-reduce | flops 1 | bytes 8 | tf_op jit(solution)/shard_map/psum | solution.py:96
  362.5 28.9 %all-reduce.7.cloned.1.call-done = f32[512,256]{1,0:T(8,128)} async-done(((f32[512,256]{1,0:T(8,128)}), f32[512,256]{1,0:T(8,128)}) %all-reduce.7.cloned.1.call-update) | async-done | bytes 524304 | tf_op jit(solution)/shard_map/psum | solution.py:88
  391.4 1.8 multiply_convert_fusion.1
  393.2 229.7 %all-reduce.5.cloned.1.call-done = bf16[512,256]{1,0:T(8,128)(2,1)} async-done(((bf16[512,256]{1,0:T(8,128)(2,1)}), bf16[512,256]{1,0:T(8,128)(2,1)}) %all-reduce.5.cloned.1.call-update) | async-done | bytes 262160 | tf_op jit(solution)/shard_map/psum | solution.py:21
  622.9 1.7 copy.51
  (90 shorter events, 10.7 us)
Async XLA Ops:
  8.0 383.4 %all-reduce.7.cloned.1.call-start = ((), (), s32[]{:S(2)}) async-start(), calls=%async_computation.2 | async-start | bytes 1048576 | tf_op jit(solution)/shard_map/psum | solution.py:88
  8.1 1.6 copy-start.1
  12.1 1.6 copy-start.1
  16.2 1.6 copy-start.1
  20.2 1.7 copy-start.1
  138.0 24.1 %copy-start.5 = (s32[512]{0:T(512)S(1)}, s32[512]{0:T(512)}, u32[]{:S(2)}) copy-start(s32[512]{0:T(512)} %param.11) | copy-start | bytes 6148
  138.0 1.9 copy-start
  138.0 1.9 copy-start.2
  140.5 1.3 copy-start.4
  143.3 1.9 copy-start
  143.3 1.9 copy-start.2
  145.7 2.4 copy-start.4
  149.5 1.9 copy-start
  149.5 1.9 copy-start.2
  151.9 2.4 copy-start.4
  155.8 1.9 copy-start
  155.8 1.9 copy-start.2
  158.2 2.4 copy-start.4
  162.0 4.6 copy-start.3
  162.1 460.8 %all-reduce.5.cloned.1.call-start = ((), (), s32[]{:S(2)}) async-start(), calls=%async_computation.1 | async-start | bytes 524288 | tf_op jit(solution)/shard_map/psum | solution.py:21
  166.5 456.4 %reduce-scatter.2.cloned.1.call-start = ((), (), s32[]{:S(2)}) async-start(), calls=%async_computation.3 | async-start | bytes 2228224 | tf_op jit(solution)/shard_map/reduce_scatter | solution.py:84
Sparse Core Ops, SparseCore 0:
  162.2 229.1 all-reduce.6
  394.9 227.9 all-reduce.4
Sparse Core Ops, SparseCore 1:
  178.4 91.6 reduce-scatter.1
where the time goes:
time: 633 us; the launch traced here: 632 us
  blocking collectives  293 us (46%)
  waiting for transfers between devices  259 us (41%)
  matrix products  36.4 us (6%)
  other arithmetic  18.4 us (3%)
  between operations  17.6 us (3%)
  local copies, waits for them, and re-layouts  7.52 us (1%)
    psum x1, waiting for transfers between devices, body(): quantized = lax.psum(picked.astype(jnp.bfloat16), 'code')  230 us
    psum x1, blocking collectives, body(): entropy_loss = lax.psum(local_loss, ('dp', 'code'))  107 us
    unnamed x1, blocking collectives  72.7 us
    pmax x1, blocking collectives, body(): row_peak = lax.pmax(local_stats[0], 'code')  59.2 us
    psum x1, blocking collectives, body(): lax.psum((local_stats[1] * rescale, local_stats[2] * rescale, local_stats...  53.9 us
    psum x1, waiting for transfers between devices, body(): token_grad = (lax.psum(running, 'code') * scale_factor).astype(jnp.bfloat16)  28.9 us
    dot_general x8, matrix products, scores(): jnp.einsum('td,kd->tk', tokens, code_block, preferred_element_type=jnp.fl...  14.2 us
  transfers between devices with their start and end apart: 3, of which 2 were waited for; matrix products, arithmetic and copies ran while one was open for 3% of the time, Pallas kernels for 0%

commit v1 on v0

--- a/solution.py
+++ b/solution.py
@@ -2,6 +2,10 @@
 import jax.numpy as jnp
 from jax import lax
 from jax.sharding import PartitionSpec as P
+
+
+def leaves_refer(arr):
+    return lax.all_gather(arr, axis_name="code").sum(axis=0)
 
 
 def body(tokens, codebook, cotangent, index):
@@ -18,7 +22,7 @@
     inside = (local_ids >= 0) & (local_ids < code_rows)
     picked = jnp.take(codebook, jnp.where(inside, local_ids, 0), axis=0)
     picked = jnp.where(inside[:, None], picked.astype(jnp.float32), 0.0)
-    quantized = lax.psum(picked.astype(jnp.bfloat16), "code")
+    quantized = leaves_refer(picked.astype(jnp.bfloat16))
     chosen_sums = jax.ops.segment_sum(
         cotangent.astype(jnp.float32),
         jnp.where(inside, local_ids, code_rows),

time: 633 us -> 482 us (0.76)
  waiting for transfers between devices: 259 us -> 104 us
    psum x1 -> x0, waiting for transfers between devices: 230 us -> none  [body(): quantized = lax.psum(picked.astype(jnp.bfloat16), 'code')]
    all_gather x0 -> x1, waiting for transfers between devices: none -> 74.7 us  [leaves_refer(): return lax.all_gather(arr, axis_name='code').sum(axis=0)]
  transfers between devices with their start and end apart: 3 -> 3, of which waited for: 2 -> 2; matrix products, arithmetic and copies ran while one was open for 3% -> 5% of each run, Pallas kernels for 0% -> 0%
where the time goes in v1:
time: 482 us; the launch traced here: 481 us
  blocking collectives  293 us (61%)
  waiting for transfers between devices  104 us (22%)
  matrix products  36.4 us (8%)
  other arithmetic  23.7 us (5%)
  between operations  17.6 us (4%)
  local copies, waits for them, and re-layouts  5.86 us (1%)
    psum x1, blocking collectives, body(): entropy_loss = lax.psum(local_loss, ('dp', 'code'))  106 us
    all_gather x1, waiting for transfers between devices, leaves_refer(): return lax.all_gather(arr, axis_name='code').sum(axis=0)  74.7 us
    unnamed x1, blocking collectives  73.5 us
    pmax x1, blocking collectives, body(): row_peak = lax.pmax(local_stats[0], 'code')  59.2 us
    psum x1, blocking collectives, body(): lax.psum((local_stats[1] * rescale, local_stats[2] * rescale, local_stats...  53.9 us
    psum x1, waiting for transfers between devices, body(): token_grad = (lax.psum(running, 'code') * scale_factor).astype(jnp.bfloat16)  29 us
    dot_general x8, matrix products, scores(): jnp.einsum('td,kd->tk', tokens, code_block, preferred_element_type=jnp.fl...  14.2 us
  transfers between devices with their start and end apart: 3, of which 2 were waited for; matrix products, arithmetic and copies ran while one was open for 5% of the time, Pallas kernels for 0%

profile of v1, /device:TPU:1, one launch (start us, length us, event | category | flops | bytes accessed | tf_op | source)
XLA Modules:
  0.0 481.0 jit_solution(11857187358249123040)
XLA Ops:
  8.1 16.1 %while.31 = (s32[]{:T(128)}, f32[4,512]{1,0:T(4,128)S(1)}, f32[4,512]{1,0:T(4,128)S(1)}, f32[4,512]{1,0:T(4,128)S(1)}, f32[4,512]{1,0:T(4,128)S(1)}, /*index=5*/...) while((s32[]{:T(128)}, f32[4,512]{1,0:T(4,128)S(1)}, ...), condition=%wide.region_6.7_spmd, body=%wide.region_1.0_spmd.sunk | while | flops 542636032 | bytes 8941729 | solution.py:51
  8.1 1.6 multiply_reduce_fusion.5
  9.8 1.6 fusion.56
  12.2 1.6 multiply_reduce_fusion.5
  13.8 1.6 fusion.56
  16.2 1.6 multiply_reduce_fusion.5
  17.8 1.6 fusion.56
  20.2 1.6 multiply_reduce_fusion.5
  21.9 1.6 fusion.56
  24.2 59.2 %pmax.7 = f32[512]{0:T(512)S(1)} all-reduce(f32[512]{0:T(512)S(1)} %reduce_max.18), channel_id=1, replica_groups=mesh['dp'=16,'code'=32] {'code'}, use_global_device_ids=true, to_apply=%region_8.9 | all-reduce | flops 512 | bytes 4096 | tf_op jit(solution)/shard_map/pmax | solution.py:60
  83.5 53.9 %all-reduce.1 = (f32[512]{0:T(512)S(1)}, f32[512]{0:T(512)S(1)}, f32[512]{0:T(512)S(1)}) all-reduce(f32[512]{0:T(512)S(1)} %get-tuple-element.198, f32[512]{0:T(512)S(1)} %get-tuple-element.197, f32[512]{0:T(512)S(1)} %get-tuple-element.196), channel_id=1, replica_groups=mesh['dp'=16,'code'=32] {'code'}, use_global_device_ids=true, to_apply=%region_10.11 | all-reduce | flops 1536 | bytes 12288 | tf_op jit(solution)/shard_map/psum | solution.py:62
  138.0 24.0 %while.32 = (s32[]{:T(128)}, f32[512,256]{1,0:T(8,128)}, f32[4,1024]{1,0:T(4,128)S(1)}, f32[4,1024,256]{2,1,0:T(8,128)}, bf16[4,1024,256]{2,1,0:T(8,128)(2,1)}, ...) while((s32[]{:T(128)}, f32[512,256]{1,0:T(8,128)}, ...), condition=%wide.region_15.16_spmd.clone, body=%wide.region_13.15_spmd.clone.sunk | while | flops 1077935104 | bytes 22300912 | solution.py:83
  138.0 1.9 fusion.64
  141.8 1.5 fusion.65
  143.3 1.9 fusion.64
  145.8 2.3 convolution_add_fusion.2
  148.1 1.4 fusion.65
  149.5 1.9 fusion.64
  152.0 2.3 convolution_add_fusion.2
  154.3 1.5 fusion.65
  155.8 1.9 fusion.64
  158.3 2.3 convolution_add_fusion.2
  160.6 1.4 fusion.65
  162.2 3.4 gather_fusion
  166.6 6.3 %scatter_custom_fusion = f32[4097,256]{1,0:T(8,128)} fusion(s32[512]{0:T(512)S(1)} %subtract_select_fusion, f32[]{:T(128)} %constant.47.clone.1, bf16[512,256]{1,0:T(8,128)(2,1)S(1)} %copy-done.3), kind=kCustom, calls=%fused_computation.34 | custom fusion | flops 262144 | bytes 4457476 | tf_op jit(solution)/shard_map/scatter-add | solution.py:26
  172.9 5.2 %fusion.22 = bf16[4096,256]{1,0:T(8,128)(2,1)} fusion(f32[4097,256]{1,0:T(8,128)} %scatter_custom_fusion, f32[4,1024,256]{2,1,0:T(8,128)} %get-tuple-element.108), kind=kLoop, calls=%fused_computation.33 | loop fusion | flops 2097152 | bytes 10485760 | tf_op jit(solution)/shard_map/convert_element_type | solution.py:89
  180.7 73.5 %all-reduce = f32[4096]{0:T(1024)S(1)} all-reduce(f32[4096]{0:T(1024)S(1)} %bitcast.109), channel_id=3, replica_groups=mesh['dp'=16,'code'=32] {'dp'}, use_global_device_ids=true, to_apply=%region_19.20.clone | all-reduce | flops 4096 | bytes 32768
  256.1 106.5 %psum.39 = f32[]{:T(128)} all-reduce(f32[]{:T(128)S(6)} %add.43), channel_id=1, replica_groups=mesh['dp'=16,'code'=32] {'dp','code'}, use_global_device_ids=true, to_apply=%region_24.25 | all-reduce | flops 1 | bytes 8 | tf_op jit(solution)/shard_map/psum | solution.py:100
  362.6 29.0 %all-reduce.4.cloned.1.call-done = f32[512,256]{1,0:T(8,128)} async-done(((f32[512,256]{1,0:T(8,128)}), f32[512,256]{1,0:T(8,128)}) %all-reduce.4.cloned.1.call-update) | async-done | bytes 524304 | tf_op jit(solution)/shard_map/psum | solution.py:92
  391.6 1.8 multiply_convert_fusion.1
  393.4 74.7 %all-gather.2.cloned.1.call-done = bf16[32,512,256]{2,1,0:T(8,128)(2,1)} async-done(((bf16[1,512,256]{2,1,0:T(8,128)(2,1)}), bf16[32,512,256]{2,1,0:T(8,128)(2,1)}) %all-gather.2.cloned.1.call-update) | async-done | bytes 8388624 | tf_op jit(solution)/shard_map/all_gather | solution.py:8
  468.1 5.5 %reduce_sum.93 = bf16[512,256]{1,0:T(8,128)(2,1)} reduce(bf16[32,512,256]{2,1,0:T(8,128)(2,1)} %all-gather.2.cloned.1.call-done, bf16[]{:T(256)} %constant.48.clone.1), dimensions={0}, to_apply=%region_0.1 | reduce | flops 4063232 | bytes 8650754 | tf_op jit(solution)/shard_map/reduce_sum | solution.py:8
  (90 shorter events, 10.7 us)
Async XLA Ops:
  8.0 383.6 %all-reduce.4.cloned.1.call-start = ((), (), s32[]{:S(2)}) async-start(), calls=%async_computation.2 | async-start | bytes 1048576 | tf_op jit(solution)/shard_map/psum | solution.py:92
  8.1 1.6 copy-start.1
  12.1 1.6 copy-start.1
  16.2 1.6 copy-start.1
  20.2 1.7 copy-start.1
  138.0 24.1 %copy-start.5 = (s32[512]{0:T(512)S(1)}, s32[512]{0:T(512)}, u32[]{:S(2)}) copy-start(s32[512]{0:T(512)} %param.11) | copy-start | bytes 6148
  138.0 1.9 copy-start
  138.0 1.9 copy-start.2
  140.5 1.3 copy-start.4
  143.3 1.9 copy-start
  143.3 1.9 copy-start.2
  145.7 2.4 copy-start.4
  149.5 1.9 copy-start
  149.5 1.9 copy-start.2
  151.9 2.4 copy-start.4
  155.8 1.9 copy-start
  155.8 1.9 copy-start.2
  158.2 2.4 copy-start.4
  162.0 4.6 copy-start.3
  162.1 306.0 %all-gather.2.cloned.1.call-start = ((), (), s32[]{:S(2)}) async-start(), calls=%async_computation.1 | async-start | bytes 8650752 | tf_op jit(solution)/shard_map/all_gather | solution.py:8
  166.5 307.0 %reduce-scatter.2.cloned.1.call-start = ((), (), s32[]{:S(2)}) async-start(), calls=%async_computation.3 | async-start | bytes 2228224 | tf_op jit(solution)/shard_map/reduce_scatter | solution.py:88
Sparse Core Ops, SparseCore 0:
  162.2 229.3 all-reduce.3
  394.3 73.7 all-gather.1
Sparse Core Ops, SparseCore 1:
  178.2 91.8 reduce-scatter.1
